TPU v7x, 256 devices: a whole 4x4x8 slice. The times are simulated.
256 devices in a mesh: seq: 4 (over x_lo, core), dp: 64 (over x_hi, y, z).
Axes of the slice: x: 4 (x_hi: 2, x_lo: 2; x = x_hi * 2 + x_lo), y: 4, z: 8, core: 2. Of those that a mesh axis runs over, the one named last changes fastest.
Arguments:
- residual: bfloat16 [49152, 2560], P(('seq', 'dp')), may hold values from -6 to 6
- query_raw: bfloat16 [49152, 2560], P(('seq', 'dp')), may hold values from -60 to 60
- key_raw: bfloat16 [49152, 2560], P(('seq', 'dp')), may hold values from -60 to 60
- values: bfloat16 [49152, 2560], P(('seq', 'dp')), may hold values from -6 to 6
- residual_grad: bfloat16 [49152, 2560], P(('seq', 'dp')), may hold values from -6 to 6
- modulated_grad: bfloat16 [49152, 2560], P(('seq', 'dp')), may hold values from -24 to 24
- condition: float32 [64, 2, 2560], P('dp'), may hold values from -3 to 3
- modulation: float32 [2, 2560], P(None, ('seq', 'dp')), may hold values from -0.5 to 0.5
- norm_gains: float32 [2, 2560], P(None, ('seq', 'dp')), may hold values from 0.25 to 1.75
Outputs:
- input_grad: bfloat16 [49152, 2560], P(('seq', 'dp'))
- query_grad: bfloat16 [49152, 2560], P(('seq', 'dp'))
- key_grad: bfloat16 [49152, 2560], P(('seq', 'dp'))
- value_grad: bfloat16 [49152, 2560], P(('seq', 'dp'))
- param_grads: float32 [5, 2560], P(None, ('seq', 'dp'))
All inputs are finite; a program needn't handle non-finite values.
Results may differ from a plain program's by a relative error of at most 0.009.
The roundings to bfloat16 on the way count: a program that leaves them out, or rounds other values in their place, can miss the bound.
Values may be sent and summed in bfloat16 or wider, within the bound.
A program may use at most 128 MiB of HBM per device.

v0:
```python
import jax
import jax.numpy as jnp
from jax import lax
from jax.sharding import PartitionSpec as P

HEAD_DIM = 128
epsilon = 1e-06


def root_scale(raw_values):
    floats = raw_values.astype(jnp.float32)
    return lax.rsqrt(jnp.mean(floats * floats, axis=1, keepdims=True) + epsilon)


def head_scores(query_head, key_head):
    return lax.dot_general(
        query_head, key_head, (((1,), (1,)), ((), ())), preferred_element_type=jnp.float32
    ) * query_head.shape[-1] ** (-0.5)


def head_forward(pieces):
    query_head, key_head, value_head = pieces
    scores = head_scores(query_head, key_head)
    row_max = jnp.max(scores, axis=1, keepdims=True)
    row_sum = jnp.sum(jnp.exp(scores - row_max), axis=1, keepdims=True)
    logsum = row_max + jnp.log(row_sum)
    weights_low = jnp.exp(scores - logsum).astype(jnp.bfloat16)
    attended = jnp.dot(weights_low, value_head, preferred_element_type=jnp.float32).astype(
        jnp.bfloat16
    )
    return (attended, logsum[:, 0])


def head_backward(pieces):
    query_head, key_head, value_head, attended, attended_grad, logsum = pieces
    scores = head_scores(query_head, key_head)
    weights = jnp.exp(scores - logsum[:, None])
    row_dot = jnp.sum(
        attended_grad.astype(jnp.float32) * attended.astype(jnp.float32), axis=1, keepdims=True
    )
    weight_grad = lax.dot_general(
        attended_grad, value_head, (((1,), (1,)), ((), ())), preferred_element_type=jnp.float32
    )
    score_grad = (weights * (weight_grad - row_dot) * query_head.shape[-1] ** (-0.5)).astype(
        jnp.bfloat16
    )
    value_part = lax.dot_general(
        weights.astype(jnp.bfloat16),
        attended_grad,
        (((0,), (0,)), ((), ())),
        preferred_element_type=jnp.float32,
    )
    query_part = jnp.dot(score_grad, key_head, preferred_element_type=jnp.float32)
    key_part = lax.dot_general(
        score_grad, query_head, (((0,), (0,)), ((), ())), preferred_element_type=jnp.float32
    )
    return (query_part, key_part, value_part)


def stream_pass(residual, attended, modulated, residual_grad, modulated_grad):
    gate_row = modulated[0]
    scale_row = modulated[1]
    summed = residual.astype(jnp.float32) + gate_row * attended.astype(jnp.float32)
    centered = summed - jnp.mean(summed, axis=1, keepdims=True)
    norm_scale = lax.rsqrt(jnp.mean(centered * centered, axis=1, keepdims=True) + epsilon)
    normed = centered * norm_scale
    scaled_grad = modulated_grad.astype(jnp.float32) * (1.0 + scale_row)
    stream_grad = residual_grad.astype(jnp.float32) + norm_scale * (
        scaled_grad
        - jnp.mean(scaled_grad, axis=1, keepdims=True)
        - normed * jnp.mean(scaled_grad * normed, axis=1, keepdims=True)
    )
    attended_grad = (stream_grad * gate_row).astype(jnp.bfloat16)
    return (stream_grad, normed, attended_grad)


def norm_backward(raw_values, inverse, gain_row, upstream):
    floats = raw_values.astype(jnp.float32)
    weighted = gain_row * upstream
    return (
        inverse * weighted
        - floats * inverse**3 * jnp.mean(floats * weighted, axis=1, keepdims=True)
    ).astype(jnp.bfloat16)


def partial_sums(
    attended,
    stream_grad,
    normed,
    modulated_grad,
    query_raw,
    query_scale,
    query_part,
    key_raw,
    key_scale,
    key_part,
):
    grad_floats = modulated_grad.astype(jnp.float32)
    return jnp.stack(
        [
            jnp.sum(stream_grad * attended.astype(jnp.float32), axis=0),
            jnp.sum(grad_floats, axis=0),
            jnp.sum(grad_floats * normed, axis=0),
            jnp.sum(query_part * query_raw.astype(jnp.float32) * query_scale, axis=0),
            jnp.sum(key_part * key_raw.astype(jnp.float32) * key_scale, axis=0),
        ]
    )


def per_device(
    residual,
    query_raw,
    key_raw,
    values,
    residual_grad,
    modulated_grad,
    condition,
    modulation,
    norm_gains,
):
    head_width = HEAD_DIM
    row_count = residual.shape[0]
    modulation_all, gains_all = (
        lax.all_gather(modulation, ("seq", "dp"), axis=1, tiled=True),
        lax.all_gather(norm_gains, ("seq", "dp"), axis=1, tiled=True),
    )
    modulated = modulation_all + condition[0]
    query_scale = root_scale(query_raw)
    key_scale = root_scale(key_raw)
    normed_query = (query_raw.astype(jnp.float32) * query_scale * gains_all[0]).astype(jnp.bfloat16)
    normed_key = (key_raw.astype(jnp.float32) * key_scale * gains_all[1]).astype(jnp.bfloat16)
    query_moved, key_moved, value_moved = (
        lax.all_to_all(
            normed_query.reshape(row_count, -1, head_width),
            "seq",
            split_axis=1,
            concat_axis=0,
            tiled=True,
        ),
        lax.all_to_all(
            normed_key.reshape(row_count, -1, head_width),
            "seq",
            split_axis=1,
            concat_axis=0,
            tiled=True,
        ),
        lax.all_to_all(
            values.reshape(row_count, -1, head_width),
            "seq",
            split_axis=1,
            concat_axis=0,
            tiled=True,
        ),
    )
    query_heads = query_moved.transpose(1, 0, 2)
    key_heads = key_moved.transpose(1, 0, 2)
    value_heads = value_moved.transpose(1, 0, 2)
    attended_heads, logsum = lax.map(head_forward, (query_heads, key_heads, value_heads))
    attended_tokens = lax.all_to_all(
        attended_heads.transpose(1, 0, 2), "seq", split_axis=0, concat_axis=1, tiled=True
    )
    attended = attended_tokens.reshape(row_count, -1)
    stream_grad, normed, attended_grad = stream_pass(
        residual, attended, modulated, residual_grad, modulated_grad
    )
    grad_moved = lax.all_to_all(
        attended_grad.reshape(row_count, -1, head_width),
        "seq",
        split_axis=1,
        concat_axis=0,
        tiled=True,
    )
    query_part, key_part, value_part = lax.map(
        head_backward,
        (
            query_heads,
            key_heads,
            value_heads,
            attended_heads,
            grad_moved.transpose(1, 0, 2),
            logsum,
        ),
    )
    query_back, key_back, value_back = (
        lax.all_to_all(
            query_part.transpose(1, 0, 2), "seq", split_axis=0, concat_axis=1, tiled=True
        ),
        lax.all_to_all(key_part.transpose(1, 0, 2), "seq", split_axis=0, concat_axis=1, tiled=True),
        lax.all_to_all(
            value_part.transpose(1, 0, 2), "seq", split_axis=0, concat_axis=1, tiled=True
        ),
    )
    query_grad_n = query_back.reshape(row_count, -1)
    key_grad_n = key_back.reshape(row_count, -1)
    value_sum = value_back.reshape(row_count, -1)
    sums_here = partial_sums(
        attended,
        stream_grad,
        normed,
        modulated_grad,
        query_raw,
        query_scale,
        query_grad_n,
        key_raw,
        key_scale,
        key_grad_n,
    )
    reduced = lax.psum_scatter(sums_here, ("seq", "dp"), scatter_dimension=1, tiled=True)
    factor = (row_count * lax.axis_size("seq") * lax.axis_size("dp")) ** (-0.5)
    return (
        stream_grad.astype(jnp.bfloat16),
        norm_backward(query_raw, query_scale, gains_all[0], query_grad_n),
        norm_backward(key_raw, key_scale, gains_all[1], key_grad_n),
        value_sum.astype(jnp.bfloat16),
        reduced * factor,
    )


def solution(mesh):
    placed = (
        P(("seq", "dp"), None),
        P(("seq", "dp"), None),
        P(("seq", "dp"), None),
        P(("seq", "dp"), None),
        P(("seq", "dp"), None),
        P(("seq", "dp"), None),
        P("dp", None, None),
        P(None, ("seq", "dp")),
        P(None, ("seq", "dp")),
    )
    return jax.shard_map(
        per_device,
        mesh=mesh,
        in_specs=placed,
        out_specs=(
            P(("seq", "dp"), None),
            P(("seq", "dp"), None),
            P(("seq", "dp"), None),
            P(("seq", "dp"), None),
            P(None, ("seq", "dp")),
        ),
        check_vma=False,
    )
```

profile of v0, /device:TPU:1, one launch (start us, length us, event | category | flops | bytes accessed | tf_op | source)
XLA Modules:
  0.0 1958.0 jit_solution(11873094181766818667)
XLA Ops:
  3.0 6.7 all-to-all-start.2
  9.8 647.2 %all-gather.1 = f32[256,10,2]{1,2,0:T(2,128)S(1)} all-gather(f32[1,10,2]{1,2,0:T(2,128)S(1)} %bitcast.194), channel_id=1, replica_groups=mesh['seq'=4,'dp'=64] {'seq','dp'}, dimensions={0}, use_global_device_ids=true | all-gather | bytes 20560 | tf_op jit(solution)/shard_map/all_gather | solution.py:125
  669.4 4.2 all-to-all-start.1
  675.9 10.5 all-to-all-done.1
  686.4 5.1 all-to-all-start
  691.5 664.9 %all-gather = f32[256,10,2]{1,2,0:T(2,128)S(1)} all-gather(f32[1,10,2]{1,2,0:T(2,128)S(1)} %bitcast.195), channel_id=1, replica_groups=mesh['seq'=4,'dp'=64] {'seq','dp'}, dimensions={0}, use_global_device_ids=true | all-gather | bytes 20560 | tf_op jit(solution)/shard_map/all_gather | solution.py:124
  1368.5 27.5 %while.26 = (s32[]{:T(128)}, bf16[5,768,128]{2,1,0:T(8,128)(2,1)}, f32[5,768]{1,0:T(8,128)}, bf16[5,768,128]{2,1,0:T(8,128)(2,1)}, bf16[5,768,128]{2,1,0:T(8,128...) while((s32[]{:T(128)}, bf16[5,768,128]{2,1,0:T(8,128)(2,1)}, f32[5,768]{1,0:T(8,128)}, ...), condition=%wide.region_5.6_spmd, body=%wide.region_2.5_spmd.sunk | while | flops 306806016 | bytes 7900257 | solution.py:158
  1399.1 4.7 all-to-all-start.3
  1403.9 19.2 all-to-all-done.3
  1438.7 4.3 all-to-all-start.4
  1443.0 12.9 all-to-all-done.4
  1457.1 218.5 %while.27 = (s32[]{:T(128)}, f32[5,768,128]{2,0,1:T(8,128)}, f32[5,768,128]{2,0,1:T(8,128)}, bf16[5,768,128]{2,0,1:T(8,128)(2,1)}, bf16[5,768,128]{2,1,0:T(8,128...) while((s32[]{:T(128)}, f32[5,768,128]{2,0,1:T(8,128)}, ...), condition=%wide.region_12.13_spmd, body=%wide.region_10.12_spmd.sunk | while | flops 760675584 | bytes 15945885 | solution.py:173
  1466.9 11.0 dynamic_update_slice.28
  1477.9 11.4 dynamic_update_slice.27
  1489.3 11.4 dynamic_update_slice.26
  1510.6 11.0 dynamic_update_slice.28
  1521.6 11.4 dynamic_update_slice.27
  1533.0 11.4 dynamic_update_slice.26
  1554.3 11.0 dynamic_update_slice.28
  1565.3 11.4 dynamic_update_slice.27
  1576.7 11.4 dynamic_update_slice.26
  1598.0 11.0 dynamic_update_slice.28
  1609.0 11.4 dynamic_update_slice.27
  1620.4 11.4 dynamic_update_slice.26
  1641.7 11.0 dynamic_update_slice.28
  1652.7 11.4 dynamic_update_slice.27
  1664.1 11.4 dynamic_update_slice.26
  1675.5 24.6 %all_to_all.120 = bf16[768,5,128]{2,1,0:T(8,128)(2,1)} all-to-all(bf16[768,5,128]{2,1,0:T(8,128)(2,1)} %bitcast.192), channel_id=1, replica_groups=mesh['seq'=4,'dp'=64] {'seq'}, dimensions={0} | all-to-all | bytes 1966080 | tf_op jit(solution)/shard_map/all_to_all | solution.py:189
  1700.1 40.3 %all_to_all.121 = f32[768,5,128]{2,1,0:T(8,128)} all-to-all(f32[768,5,128]{2,1,0:T(8,128)S(1)} %bitcast.191), channel_id=1, replica_groups=mesh['seq'=4,'dp'=64] {'seq'}, dimensions={0} | all-to-all | bytes 3932160 | tf_op jit(solution)/shard_map/all_to_all | solution.py:185
  1740.4 5.6 all-to-all-start.6
  1756.7 25.5 %all-to-all-done.6 = f32[768,5,128]{2,1,0:T(8,128)} async-done(((f32[768,5,128]{2,1,0:T(8,128)}), f32[768,5,128]{2,1,0:T(8,128)}, u32[]{:S(2)}, u32[]{:S(2)}) %all-to-all-start.6) | async-done | bytes 1966112 | tf_op jit(solution)/shard_map/all_to_all | solution.py:188
  1800.0 157.2 %all-reduce = f32[5,2560]{1,0:T(8,128)S(1)} all-reduce(f32[5,2560]{1,0:T(8,128)S(1)} %stack.23), channel_id=2, replica_groups=mesh['seq'=4,'dp'=64] {'seq','dp'}, use_global_device_ids=true, to_apply=%region_20.21.clone | all-reduce | flops 12800 | bytes 102400
  (168 shorter events, 154.7 us)
Async XLA Ops:
  0.6 1.2 copy-start
  0.6 9.1 copy-start.18
  0.7 656.6 %copy-start.9 = (bf16[192,2560]{1,0:T(8,128)(2,1)S(1)}, bf16[192,2560]{1,0:T(8,128)(2,1)}, u32[]{:S(2)}) copy-start(bf16[192,2560]{1,0:T(8,128)(2,1)} %param.14) | copy-start | bytes 2949124
  3.0 666.3 %all-to-all-start.2 = ((bf16[192,20,128]{2,0,1:T(8,128)(2,1)}), bf16[192,20,128]{2,0,1:T(8,128)(2,1)S(1)}, u32[]{:S(2)}, u32[]{:S(2)}) async-start(bf16[192,20,128]{2,0,1:T(8,128)(2,1)} %copy_bitcast_fusion.1), calls=%async_computation.2 | async-start | bytes 1966080 | tf_op jit(solution)/shard_map/all_to_all | solution.py:147
  657.2 6.3 copy-start.10
  663.5 3.5 copy-start.14
  669.4 17.1 all-to-all-start.1
  673.5 18.0 copy-start.19
  686.4 679.9 %all-to-all-start = ((bf16[192,20,128]{2,0,1:T(8,128)(2,1)}), bf16[192,20,128]{2,0,1:T(8,128)(2,1)}, u32[]{:S(2)}, u32[]{:S(2)}) async-start(bf16[192,20,128]{2,0,1:T(8,128)(2,1)} %copy.75), calls=%async_computation | async-start | bytes 1966080 | tf_op jit(solution)/shard_map/all_to_all | solution.py:133
  1396.0 7.8 copy-start.12
  1396.0 7.8 copy-start.13
  1399.1 24.0 %all-to-all-start.3 = ((bf16[768,5,128]{2,1,0:T(8,128)(2,1)}), bf16[768,5,128]{2,1,0:T(8,128)(2,1)}, u32[]{:S(2)}, u32[]{:S(2)}) async-start(bf16[768,5,128]{2,1,0:T(8,128)(2,1)} %bitcast.181), calls=%async_computation.3 | async-start | bytes 3145728 | tf_op jit(solution)/shard_map/all_to_all | solution.py:159
  1428.8 1.3 copy-start.6
  1429.2 3.0 copy-start.5
  1429.2 3.0 copy-start.7
  1438.7 17.2 all-to-all-start.4
  1675.5 24.6 %copy-start.8 = (f32[5,768,128]{2,0,1:T(8,128)S(1)}, f32[5,768,128]{2,0,1:T(8,128)}, u32[]{:S(2)}) copy-start(f32[5,768,128]{2,0,1:T(8,128)} %get-tuple-element.94) | copy-start | bytes 5898244
  1740.4 41.8 %all-to-all-start.6 = ((f32[768,5,128]{2,1,0:T(8,128)}), f32[768,5,128]{2,1,0:T(8,128)}, u32[]{:S(2)}, u32[]{:S(2)}) async-start(f32[768,5,128]{2,1,0:T(8,128)} %bitcast.190), calls=%async_computation.6 | async-start | bytes 6291456 | tf_op jit(solution)/shard_map/all_to_all | solution.py:188
  1782.2 3.4 copy-start.11
  1782.2 3.4 copy-start.15
  1785.6 3.4 copy-start.2
  1785.6 3.4 copy-start.4
  1785.6 3.4 copy-start.17
  1790.6 5.3 copy-start.16
  1793.0 3.0 copy-start.3
  1795.9 162.0 %copy-start.1 = (bf16[192,2560]{1,0:T(8,128)(2,1)S(1)}, bf16[192,2560]{1,0:T(8,128)(2,1)}, u32[]{:S(2)}) copy-start(bf16[192,2560]{1,0:T(8,128)(2,1)} %param.16) | copy-start | bytes 2949124
where the time goes:
time: 1960 us
  blocking collectives  1530 us (78%)
  local copies, waits for them, and re-layouts  232 us (12%)
  waiting for transfers between devices  68.1 us (3%)
  matrix products  57.8 us (3%)
  other arithmetic  34.3 us (2%)
  starting transfers between devices  30.7 us (2%)
    all_gather x1, blocking collectives, per_device(): lax.all_gather(modulation, ('seq', 'dp'), axis=1, tiled=True)  665 us
    all_gather x1, blocking collectives, per_device(): lax.all_gather(norm_gains, ('seq', 'dp'), axis=1, tiled=True)  647 us
    dynamic_update_slice x15, local copies, waits for them, and re-layouts, per_device(): lax.map(head_backward, (query_heads, key_heads, value_heads, attended_hea...  169 us
    unnamed x1, blocking collectives  157 us
    all_to_all x1, blocking collectives, per_device(): lax.all_to_all(query_part.transpose(1, 0, 2), 'seq', split_axis=0, concat...  40.3 us
  transfers between devices with their start and end apart: 6, of which 4 were waited for; matrix products, arithmetic and copies ran while one was open for 2% of the time, Pallas kernels for 0%

commit v1 on v0

--- a/solution.py
+++ b/solution.py
@@ -121,7 +121,12 @@
     head_width = HEAD_DIM
     row_count = residual.shape[0]
     modulation_all, gains_all = (
-        lax.all_gather(modulation, ("seq", "dp"), axis=1, tiled=True),
+        jnp.concatenate(
+            lax.all_to_all(
+                jnp.stack([modulation] * lax.axis_size(("seq", "dp"))), ("seq", "dp"), 0, 0
+            ),
+            axis=1,
+        ),
         lax.all_gather(norm_gains, ("seq", "dp"), axis=1, tiled=True),
     )
     modulated = modulation_all + condition[0]

time: 1960 us -> 1290 us (0.66)
  blocking collectives: 1530 us -> 841 us
    all_gather x1 -> x0, blocking collectives: 665 us -> none  [per_device(): lax.all_gather(modulation, ('seq', 'dp'), axis=1, tiled=True)]
    unnamed x1, blocking collectives: 157 us -> 128 us
  transfers between devices with their start and end apart: 6 -> 7, of which waited for: 4 -> 6; matrix products, arithmetic and copies ran while one was open for 2% -> 3% of each run, Pallas kernels for 0% -> 0%
where the time goes in v1:
time: 1290 us
  blocking collectives  841 us (65%)
  local copies, waits for them, and re-layouts  233 us (18%)
  waiting for transfers between devices  77 us (6%)
  matrix products  57.8 us (4%)
  starting transfers between devices  43.8 us (3%)
  other arithmetic  34.3 us (3%)
    all_gather x1, blocking collectives, per_device(): lax.all_gather(norm_gains, ('seq', 'dp'), axis=1, tiled=True)  648 us
    dynamic_update_slice x15, local copies, waits for them, and re-layouts, per_device(): lax.map(head_backward, (query_heads, key_heads, value_heads, attended_hea...  169 us
    unnamed x1, blocking collectives  128 us
    all_to_all x1, blocking collectives, per_device(): lax.all_to_all(query_part.transpose(1, 0, 2), 'seq', split_axis=0, concat...  40.3 us
  transfers between devices with their start and end apart: 7, of which 6 were waited for; matrix products, arithmetic and copies ran while one was open for 3% of the time, Pallas kernels for 0%

profile of v1, /device:TPU:1, one launch (start us, length us, event | category | flops | bytes accessed | tf_op | source)
XLA Modules:
  0.0 1287.7 jit_solution(9550166034077311525)
XLA Ops:
  2.2 15.7 %all-to-all-start = ((f32[256,2,10]{2,1,0:T(2,128)}), f32[256,2,10]{2,1,0:T(2,128)S(1)}, u32[]{:S(2)}, u32[]{:S(2)}) async-start(f32[256,2,10]{2,1,0:T(2,128)} %stack.14), calls=%async_computation | async-start | bytes 524288 | tf_op jit(solution)/shard_map/all_to_all | solution.py:125
  17.8 648.1 %all-gather = f32[256,10,2]{1,2,0:T(2,128)S(1)} all-gather(f32[1,10,2]{1,2,0:T(2,128)} %bitcast.189), channel_id=1, replica_groups=mesh['seq'=4,'dp'=64] {'seq','dp'}, dimensions={0}, use_global_device_ids=true | all-gather | bytes 20560 | tf_op jit(solution)/shard_map/all_gather | solution.py:130
  682.7 6.9 all-to-all-done.3
  689.6 4.4 all-to-all-start.2
  696.3 10.5 all-to-all-done.2
  706.9 5.1 all-to-all-start.1
  727.2 27.4 %while.26 = (s32[]{:T(128)}, bf16[5,768,128]{2,1,0:T(8,128)(2,1)}, f32[5,768]{1,0:T(8,128)}, bf16[5,768,128]{2,1,0:T(8,128)(2,1)}, bf16[5,768,128]{2,1,0:T(8,128...) while((s32[]{:T(128)}, bf16[5,768,128]{2,1,0:T(8,128)(2,1)}, f32[5,768]{1,0:T(8,128)}, ...), condition=%wide.region_5.6_spmd, body=%wide.region_2.5_spmd.sunk | while | flops 306806016 | bytes 7900257 | solution.py:163
  757.7 5.2 all-to-all-start.4
  763.0 19.2 %all-to-all-done.4 = bf16[768,5,128]{2,1,0:T(8,128)(2,1)} async-done(((bf16[768,5,128]{2,1,0:T(8,128)(2,1)}), bf16[768,5,128]{2,1,0:T(8,128)(2,1)}, u32[]{:S(2)}, u32[]{:S(2)}) %all-to-all-start.4) | async-done | bytes 983072 | tf_op jit(solution)/shard_map/all_to_all | solution.py:164
  797.8 4.3 all-to-all-start.5
  802.1 12.9 %all-to-all-done.5 = bf16[192,20,128]{2,0,1:T(8,128)(2,1)S(1)} async-done(((bf16[192,20,128]{2,0,1:T(8,128)(2,1)}), bf16[192,20,128]{2,0,1:T(8,128)(2,1)S(1)}, u32[]{:S(2)}, u32[]{:S(2)}) %all-to-all-start.5) | async-done | bytes 983072 | tf_op jit(solution)/shard_map/all_to_all | solution.py:171
  816.1 218.5 %while.27 = (s32[]{:T(128)}, f32[5,768,128]{2,0,1:T(8,128)}, f32[5,768,128]{2,0,1:T(8,128)}, bf16[5,768,128]{2,0,1:T(8,128)(2,1)}, bf16[5,768,128]{2,1,0:T(8,128...) while((s32[]{:T(128)}, f32[5,768,128]{2,0,1:T(8,128)}, ...), condition=%wide.region_12.13_spmd, body=%wide.region_10.12_spmd.sunk | while | flops 760675584 | bytes 15945885 | solution.py:178
  826.0 11.0 dynamic_update_slice.28
  837.0 11.4 dynamic_update_slice.27
  848.4 11.4 dynamic_update_slice.26
  869.7 11.0 dynamic_update_slice.28
  880.7 11.4 dynamic_update_slice.27
  892.1 11.4 dynamic_update_slice.26
  913.4 11.0 dynamic_update_slice.28
  924.4 11.4 dynamic_update_slice.27
  935.8 11.4 dynamic_update_slice.26
  957.1 11.0 dynamic_update_slice.28
  968.1 11.4 dynamic_update_slice.27
  979.5 11.4 dynamic_update_slice.26
  1000.8 11.0 dynamic_update_slice.28
  1011.8 11.4 dynamic_update_slice.27
  1023.2 11.4 dynamic_update_slice.26
  1034.6 24.5 %all_to_all.125 = bf16[768,5,128]{2,1,0:T(8,128)(2,1)} all-to-all(bf16[768,5,128]{2,1,0:T(8,128)(2,1)} %bitcast.186), channel_id=1, replica_groups=mesh['seq'=4,'dp'=64] {'seq'}, dimensions={0} | all-to-all | bytes 1966080 | tf_op jit(solution)/shard_map/all_to_all | solution.py:194
  1059.2 40.3 %all_to_all.126 = f32[768,5,128]{2,1,0:T(8,128)} all-to-all(f32[768,5,128]{2,1,0:T(8,128)S(1)} %bitcast.185), channel_id=1, replica_groups=mesh['seq'=4,'dp'=64] {'seq'}, dimensions={0} | all-to-all | bytes 3932160 | tf_op jit(solution)/shard_map/all_to_all | solution.py:190
  1099.4 5.6 all-to-all-start.7
  1115.7 25.5 %all-to-all-done.7 = f32[768,5,128]{2,1,0:T(8,128)} async-done(((f32[768,5,128]{2,1,0:T(8,128)}), f32[768,5,128]{2,1,0:T(8,128)}, u32[]{:S(2)}, u32[]{:S(2)}) %all-to-all-start.7) | async-done | bytes 1966112 | tf_op jit(solution)/shard_map/all_to_all | solution.py:193
  1159.1 128.0 %all-reduce = f32[5,2560]{1,0:T(8,128)S(1)} all-reduce(f32[5,2560]{1,0:T(8,128)S(1)} %stack.20), channel_id=2, replica_groups=mesh['seq'=4,'dp'=64] {'seq','dp'}, use_global_device_ids=true, to_apply=%region_20.21.clone | all-reduce | flops 12800 | bytes 102400
  (168 shorter events, 161.3 us)
Async XLA Ops:
  0.6 666.1 %copy-start = (bf16[192,2560]{1,0:T(8,128)(2,1)S(1)}, bf16[192,2560]{1,0:T(8,128)(2,1)}, u32[]{:S(2)}) copy-start(bf16[192,2560]{1,0:T(8,128)(2,1)} %param.16) | copy-start | bytes 2949124
  2.2 671.1 %all-to-all-start = ((f32[256,2,10]{2,1,0:T(2,128)}), f32[256,2,10]{2,1,0:T(2,128)S(1)}, u32[]{:S(2)}, u32[]{:S(2)}) async-start(f32[256,2,10]{2,1,0:T(2,128)} %stack.14), calls=%async_computation | async-start | bytes 524288 | tf_op jit(solution)/shard_map/all_to_all | solution.py:125
  666.7 1.2 copy-start.9
  668.0 1.6 copy-start.10
  668.5 4.7 copy-start.13
  673.3 7.1 copy-start.15
  673.3 7.1 copy-start.11
  673.3 16.3 %all-to-all-start.3 = ((bf16[192,20,128]{2,0,1:T(8,128)(2,1)}), bf16[192,20,128]{2,0,1:T(8,128)(2,1)S(1)}, u32[]{:S(2)}, u32[]{:S(2)}) async-start(bf16[192,20,128]{2,0,1:T(8,128)(2,1)} %copy_bitcast_fusion.1), calls=%async_computation.3 | async-start | bytes 1966080 | tf_op jit(solution)/shard_map/all_to_all | solution.py:152
  689.6 17.2 %all-to-all-start.2 = ((bf16[192,20,128]{2,0,1:T(8,128)(2,1)}), bf16[192,20,128]{2,0,1:T(8,128)(2,1)S(1)}, u32[]{:S(2)}, u32[]{:S(2)}) async-start(bf16[192,20,128]{2,0,1:T(8,128)(2,1)} %copy.77), calls=%async_computation.2 | async-start | bytes 1966080 | tf_op jit(solution)/shard_map/all_to_all | solution.py:145
  706.9 18.1 %all-to-all-start.1 = ((bf16[192,20,128]{2,0,1:T(8,128)(2,1)}), bf16[192,20,128]{2,0,1:T(8,128)(2,1)}, u32[]{:S(2)}, u32[]{:S(2)}) async-start(bf16[192,20,128]{2,0,1:T(8,128)(2,1)} %copy.73), calls=%async_computation.1 | async-start | bytes 1966080 | tf_op jit(solution)/shard_map/all_to_all | solution.py:138
  754.6 8.3 copy-start.14
  757.7 24.5 %all-to-all-start.4 = ((bf16[768,5,128]{2,1,0:T(8,128)(2,1)}), bf16[768,5,128]{2,1,0:T(8,128)(2,1)}, u32[]{:S(2)}, u32[]{:S(2)}) async-start(bf16[768,5,128]{2,1,0:T(8,128)(2,1)} %bitcast.175), calls=%async_computation.4 | async-start | bytes 3145728 | tf_op jit(solution)/shard_map/all_to_all | solution.py:164
  787.9 1.3 copy-start.6
  788.3 3.0 copy-start.5
  788.3 3.0 copy-start.7
  797.8 17.2 %all-to-all-start.5 = ((bf16[192,20,128]{2,0,1:T(8,128)(2,1)}), bf16[192,20,128]{2,0,1:T(8,128)(2,1)S(1)}, u32[]{:S(2)}, u32[]{:S(2)}) async-start(bf16[192,20,128]{2,0,1:T(8,128)(2,1)} %copy.85), calls=%async_computation.5 | async-start | bytes 1966080 | tf_op jit(solution)/shard_map/all_to_all | solution.py:171
  1034.6 24.5 %copy-start.8 = (f32[5,768,128]{2,0,1:T(8,128)S(1)}, f32[5,768,128]{2,0,1:T(8,128)}, u32[]{:S(2)}) copy-start(f32[5,768,128]{2,0,1:T(8,128)} %get-tuple-element.94) | copy-start | bytes 5898244
  1099.4 41.8 %all-to-all-start.7 = ((f32[768,5,128]{2,1,0:T(8,128)}), f32[768,5,128]{2,1,0:T(8,128)}, u32[]{:S(2)}, u32[]{:S(2)}) async-start(f32[768,5,128]{2,1,0:T(8,128)} %bitcast.184), calls=%async_computation.7 | async-start | bytes 6291456 | tf_op jit(solution)/shard_map/all_to_all | solution.py:193
  1141.2 3.4 copy-start.12
  1141.2 3.4 copy-start.16
  1144.6 3.4 copy-start.2
  1144.6 3.4 copy-start.4
  1144.6 3.4 copy-start.18
  1149.7 5.3 copy-start.17
  1152.0 3.0 copy-start.3
  1155.0 132.8 %copy-start.1 = (bf16[192,2560]{1,0:T(8,128)(2,1)S(1)}, bf16[192,2560]{1,0:T(8,128)(2,1)}, u32[]{:S(2)}) copy-start(bf16[192,2560]{1,0:T(8,128)(2,1)} %param.16) | copy-start | bytes 2949124
